TPU v7x, 32 devices: a whole 2x2x4 slice. The times are simulated.
32 devices in a mesh: rep: 2 (over y), ep: 8 (over z, core), tp: 2 (over x).
Axes of the slice: x: 2, y: 2, z: 4, core: 2. Of those that a mesh axis runs over, the one named last changes fastest.
Arguments:
- hidden_states: bfloat16 [2, 1024, 2048], P(None, ('rep', 'ep'), 'tp'), parts along dimension 1, may hold values from -8 to 8
- queries: bfloat16 [2, 1024, 4096], P(None, ('rep', 'ep'), 'tp'), parts along dimension 1, may hold values from -8 to 8
- fresh_key_value: bfloat16 [2, 1024, 2, 512], P(None, ('rep', 'ep'), None, 'tp'), parts along dimension 1, may hold values from -8 to 8
- cache: bfloat16 [16, 2, 1024, 512], P(('rep', 'ep'), None, None, 'tp'), parts along dimension 0, may hold values from -8 to 8
- cache_lengths: int32 [16], P(('rep', 'ep')), parts along dimension 0, may hold values from 1 to 1024, 4096 in all
- out_weight: bfloat16 [4096, 2048], P('tp', 'ep'), may hold values from -1 to 1
- router_weight: bfloat16 [2048, 16], P('tp'), may hold values from -0.125 to 0.125
- expert_weights: bfloat16 [16, 3, 2048, 384], P('ep', None, 'tp'), may hold values from -0.21875 to 0.21875
- expert_ids: int32 [2, 1024, 8], P(None, ('rep', 'ep')), parts along dimension 1, may hold values from 0 to 15, all different within a row; in each aligned block of 64 rows (0 to 63, 64 to 127, ..., all dimensions but the last counted through in order) at most 48 rows name the same one
- old_slots: int32 [16], replicated, may hold values from 0 to 15, as said below
- new_slots: int32 [16], replicated, may hold values from 0 to 15, as said below
- moved_experts: int32 [4], replicated, may hold values from 0 to 15, as said below
Outputs:
- mixed: bfloat16 [2, 1024, 2048], P(None, ('rep', 'ep'), 'tp'), parts along dimension 1
There are 2 independent parts, one for each index of `rep`. A program takes and returns all parts, laid end to end along the dimension named above; an argument that names none is the same for every part. Nothing has to cross between parts.
Inputs may be any that keep to these rules, and one draw needn't show every extreme that they name: `expert_ids`: each row names 8 different experts. Within the 64 rows of one request in one token block, no expert is named by more than 48 rows, a bound that some block reaches. `old_slots`: A permutation: each slot holds one expert. `new_slots`: equal to old_slots except at the moved experts, which take one another's old slots, none keeping its own. `moved_experts`: 4 different experts; no two of their old slots s share the same s // 2.
All inputs are finite; a program needn't handle non-finite values. No bound on the sum of `cache_lengths` on one device may be relied on, other than what follows from the above.
Results may differ from a plain program's by a relative error of at most 0.017.
Values may be sent and summed in bfloat16 or wider, within the bound.
A program may use at most 64 MiB of HBM per device.

v0:
```python
import jax
import jax.numpy as jnp
from jax import lax
from jax.sharding import PartitionSpec as P

D = 2048
HEAD_SIZE = 128


def lookup(entries, wanted_keys):
    return jnp.sum(
        jnp.where(
            wanted_keys[..., None] == jnp.arange(entries.shape[0], dtype=jnp.int32), entries, 0
        ),
        -1,
    )


def attend_local(queries, fresh_key_value, cache, cache_lengths):
    tokens_dev = queries.shape[1]
    kv_heads = fresh_key_value.shape[3] // HEAD_SIZE
    query_group_width = queries.shape[2] // HEAD_SIZE // kv_heads
    key_matrix = jnp.concatenate(
        [cache[0, 0], fresh_key_value[0, :, 0], fresh_key_value[1, :, 0]], 0
    )
    value_matrix = jnp.concatenate(
        [cache[0, 1], fresh_key_value[0, :, 1], fresh_key_value[1, :, 1]], 0
    )
    key_total = key_matrix.shape[0]
    context = cache.shape[2]
    query_matrix = queries.reshape(2 * tokens_dev, kv_heads, query_group_width, HEAD_SIZE)
    attention_scores = jnp.einsum(
        "meqt,wet->eqmw",
        query_matrix,
        key_matrix.reshape(key_total, kv_heads, HEAD_SIZE),
        preferred_element_type=jnp.float32,
    ) * HEAD_SIZE ** (-0.5)
    position = jnp.arange(key_total, dtype=jnp.int32)[None, :]
    row_index = jnp.arange(2 * tokens_dev, dtype=jnp.int32)[:, None]
    visible = jnp.where(
        position < context, position < cache_lengths[0], position - context <= row_index
    )
    attention_scores = jnp.where(visible, attention_scores, jnp.float32(-1e30))
    largest = jnp.max(attention_scores, -1, keepdims=True)
    weights = jnp.where(visible, jnp.exp(attention_scores - largest), jnp.float32(0.0))
    route_probability = (weights / jnp.sum(weights, -1, keepdims=True)).astype(jnp.bfloat16)
    layer_result = jnp.einsum(
        "qizo,oqx->zqix",
        route_probability,
        value_matrix.reshape(key_total, kv_heads, HEAD_SIZE),
        preferred_element_type=jnp.float32,
    )
    return layer_result.reshape(2 * tokens_dev, -1).astype(jnp.bfloat16)


def run_slots(weights, received):
    gate_up = jnp.einsum(
        "secq,egqf->secgf", received, weights[:, :2], preferred_element_type=jnp.float32
    )
    summed = lax.psum(gate_up.astype(jnp.bfloat16), "tp").astype(jnp.float32)
    hidden = (jax.nn.silu(summed[:, :, :, 0]) * summed[:, :, :, 1]).astype(jnp.bfloat16)
    layer_result = jnp.einsum(
        "secf,eqf->secq", hidden, weights[:, 2], preferred_element_type=jnp.float32
    ).astype(jnp.bfloat16)
    return lax.all_to_all(layer_result, "ep", split_axis=0, concat_axis=0, tiled=True)


def mix_block(normed_rows, resid_rows, routed, combine, slot_table, weights, capacity, groups):
    tokens_dev, top_count = routed.shape
    experts = slot_table.shape[0]
    local_slots = weights.shape[0]
    quarter = normed_rows.shape[1]
    slot_index = lookup(slot_table, routed)
    picked_mask = routed[:, :, None] == jnp.arange(experts, dtype=jnp.int32)[None, None, :]
    expert_marks = picked_mask.any(1).astype(jnp.bfloat16)
    earlier = (jnp.arange(tokens_dev)[:, None] > jnp.arange(tokens_dev)[None, :]).astype(
        jnp.bfloat16
    )
    before = jnp.dot(earlier, expert_marks, preferred_element_type=jnp.float32)
    slot_rank = jnp.sum(jnp.where(picked_mask, before[:, None, :], 0.0), -1).astype(jnp.int32)
    buffer_row = (slot_index * capacity + slot_rank).reshape(-1)
    buffer_rows = (
        jnp.zeros((groups * local_slots * capacity, quarter), jnp.bfloat16)
        .at[buffer_row]
        .set(jnp.repeat(normed_rows, top_count, axis=0))
    )
    outgoing = buffer_rows.reshape(groups, local_slots, capacity, quarter)
    returned = run_slots(
        weights, lax.all_to_all(outgoing, "ep", split_axis=0, concat_axis=0, tiled=True)
    )
    gathered = returned.reshape(-1, quarter)[buffer_row].reshape(tokens_dev, top_count, quarter)
    mixed_rows = resid_rows.astype(jnp.float32) + jnp.sum(
        combine[:, :, None] * gathered.astype(jnp.float32), 1
    )
    return mixed_rows.astype(jnp.bfloat16)


def relocate(expert_weights, old_slots, new_slots, moved_experts):
    local_slots = expert_weights.shape[0]
    groups = lax.axis_size("ep")
    flat_weights = expert_weights.reshape(local_slots, groups, -1)
    old_moved = lookup(old_slots, moved_experts)
    new_moved = lookup(new_slots, moved_experts)
    own_slots = lax.axis_index("ep") * local_slots + jnp.arange(local_slots, dtype=jnp.int32)
    leaving = (own_slots[:, None] == old_moved[None, :]).any(1)
    outgoing = jnp.sum(jnp.where(leaving[:, None, None], flat_weights, jnp.bfloat16(0.0)), 0)
    spread = lax.all_to_all(outgoing, "ep", split_axis=0, concat_axis=0, tiled=True)
    target_dev = new_moved // local_slots
    anchor_dev = old_moved // local_slots
    matches = jnp.arange(groups, dtype=jnp.int32)[:, None] == target_dev[None, :]
    anchor = jnp.sum(jnp.where(matches, anchor_dev[None, :], 0), 1)
    picked = jnp.where(matches.any(1)[:, None], spread[anchor], jnp.bfloat16(0.0))
    landed = lax.all_to_all(picked, "ep", split_axis=0, concat_axis=0, tiled=True)
    arriving = (own_slots[:, None] == new_moved[None, :]).any(1)
    return jnp.where(
        arriving[:, None, None, None],
        landed.reshape(expert_weights.shape[1:])[None],
        expert_weights,
    )


def per_device(
    hidden_states,
    queries,
    fresh_key_value,
    cache,
    cache_lengths,
    out_weight,
    router_weight,
    expert_weights,
    expert_ids,
    old_slots,
    new_slots,
    moved_experts,
):
    tokens_dev = hidden_states.shape[1]
    quarter = hidden_states.shape[2]
    experts = router_weight.shape[1]
    top_count = expert_ids.shape[2]
    groups = lax.axis_size("ep")
    capacity = min(tokens_dev, 3 * tokens_dev * top_count // (2 * experts))
    attention = attend_local(queries, fresh_key_value, cache, cache_lengths)
    head_terms = jnp.dot(
        attention,
        lax.all_gather(out_weight, "ep", axis=1, tiled=True),
        preferred_element_type=jnp.float32,
    )
    attn_out = lax.psum_scatter(
        head_terms.astype(jnp.bfloat16), "tp", scatter_dimension=1, tiled=True
    ).astype(jnp.float32)
    residual = (
        hidden_states.reshape(2 * tokens_dev, quarter).astype(jnp.float32) + attn_out
    ).astype(jnp.bfloat16)
    wide = residual.astype(jnp.float32)
    squares = lax.psum(jnp.sum(wide * wide, 1), "tp")
    normed = (wide * lax.rsqrt(squares / D + 1e-06)[:, None]).astype(jnp.bfloat16)
    logits = lax.psum(
        jnp.dot(normed, router_weight, preferred_element_type=jnp.float32).astype(jnp.bfloat16),
        "tp",
    ).astype(jnp.float32)
    routed = expert_ids.reshape(2 * tokens_dev, top_count)
    selected = jnp.sum(
        jnp.where(
            routed[:, :, None] == jnp.arange(experts, dtype=jnp.int32)[None, None, :],
            logits[:, None, :],
            0.0,
        ),
        -1,
    )
    raised = jnp.exp(selected)
    combine = raised / jnp.sum(raised, 1, keepdims=True)
    weights_two = relocate(expert_weights, old_slots, new_slots, moved_experts)
    outputs = []
    for block_index, slot_table, weights in (
        (0, old_slots, expert_weights),
        (1, new_slots, weights_two),
    ):
        lower = block_index * tokens_dev
        upper = lower + tokens_dev
        outputs.append(
            mix_block(
                normed[lower:upper],
                residual[lower:upper],
                routed[lower:upper],
                combine[lower:upper],
                slot_table,
                weights,
                capacity,
                groups,
            )
        )
    return jnp.stack(outputs)


def solution(mesh):
    return jax.shard_map(
        per_device,
        mesh=mesh,
        in_specs=(
            P(None, ("rep", "ep"), "tp"),
            P(None, ("rep", "ep"), "tp"),
            P(None, ("rep", "ep"), None, "tp"),
            P(("rep", "ep"), None, None, "tp"),
            P(("rep", "ep")),
            P("tp", "ep"),
            P("tp", None),
            P("ep", None, "tp", None),
            P(None, ("rep", "ep"), None),
            P(),
            P(),
            P(),
        ),
        out_specs=P(None, ("rep", "ep"), "tp"),
        check_vma=False,
    )
```

profile of v0, /device:TPU:0, one launch (start us, length us, event | category | flops | bytes accessed | tf_op | source)
XLA Modules:
  0.0 492.9 jit_solution(13353196676988205239)
XLA Ops:
  7.6 4.8 select_reduce_fusion
  12.4 3.9 all_to_all.32
  17.0 15.5 %reduce.7 = bf16[8,147456]{1,0:T(8,128)(2,1)S(1)} reduce(bf16[8,1,147456]{2,1,0:T(2,128)(2,1)} %all_to_all.32, bf16[]{:T(256)} %broadcast.258), dimensions={1}, to_apply=%all_to_all.32.reduce_sub_computation | reduce | bytes 4718594 | tf_op jit(solution)/shard_map/all_to_all | solution.py:107
  36.0 6.4 %all-to-all-start.2 = ((bf16[8,2,73728]{2,1,0:T(2,128)(2,1)}), bf16[8,2,73728]{2,1,0:T(2,128)(2,1)S(1)}, u32[]{:S(2)}, u32[]{:S(2)}) async-start(bf16[8,2,73728]{2,1,0:T(2,128)(2,1)} %reshape.319), calls=%async_computation.3 | async-start | bytes 4718592 | tf_op jit(solution)/shard_map/all_to_all | solution.py:107
  53.9 9.2 %fusion.94 = (f32[2,8,128]{2,1,0:T(8,128)}, f32[2,8,128,1152]{2,3,1,0:T(8,128)}) fusion(pred[128,1152]{0,1:T(8,128)(4,1)} %fusion.61, bf16[128,2,8,128]{3,2,1,0:T(8,128)(2,1)S(1)} %bitcast.180, bf16[64,2,128]{2,0,1:T(8,128)(2,1)S(1)} %get-tuple-element.35, bf16[64,2,128]{2,0,1:T(8,128)(2,1)} %get-tuple-element.36, bf16[1024,2,128]{2,0,1:T(8,128)(2,1)} %copy.102), kind=kOutput, calls=%fused_computation.146 | convolution fusion | flops 617546880 | bytes 10706944 | tf_op jit(solution)/shard_map/sub | solution.py:45
  63.1 86.6 %all-to-all-done.2 = bf16[8,2,73728]{2,1,0:T(2,128)(2,1)S(1)} async-done(((bf16[8,2,73728]{2,1,0:T(2,128)(2,1)}), bf16[8,2,73728]{2,1,0:T(2,128)(2,1)S(1)}, u32[]{:S(2)}, u32[]{:S(2)}) %all-to-all-start.2) | async-done | bytes 2359328 | tf_op jit(solution)/shard_map/all_to_all | solution.py:107
  149.6 4.6 reshape.320
  154.2 5.4 %copy.171 = bf16[8,1,147456]{2,0,1:T(8,128)(2,1)S(1)} copy(bf16[8,1,147456]{2,1,0:T(2,128)(2,1)} %reshape.320) | data formatting | bytes 4718592
  170.7 5.2 %reshape.321 = bf16[8,2,73728]{2,1,0:T(2,128)(2,1)} reshape(bf16[8,147456]{1,0:T(8,128)(2,1)} %reduce.8) | data formatting | bytes 4718592
  175.9 6.2 %all-to-all-start.3 = ((bf16[8,2,73728]{2,1,0:T(2,128)(2,1)}), bf16[8,2,73728]{2,1,0:T(2,128)(2,1)S(1)}, u32[]{:S(2)}, u32[]{:S(2)}) async-start(bf16[8,2,73728]{2,1,0:T(2,128)(2,1)} %reshape.321), calls=%async_computation.4 | async-start | bytes 4718592 | tf_op jit(solution)/shard_map/all_to_all | solution.py:113
  185.1 4.6 fusion.45
  189.7 5.5 %convolution_convert_fusion = bf16[128,2048]{1,0:T(8,128)(2,1)} fusion(bf16[128,2048]{0,1:T(8,128)(2,1)S(1)} %bitcast.178, bf16[2048,2048]{1,0:T(8,128)(2,1)} %all-gather.2.cloned.1.call-done), kind=kOutput, calls=%fused_computation.23 | convolution fusion | flops 1074003968 | bytes 9437184 | tf_op jit(solution)/shard_map/dot_general | solution.py:143
  195.9 15.5 %reduce-scatter.2.cloned.1.call-done = bf16[128,1024]{1,0:T(8,128)(2,1)} async-done(((bf16[128,2048]{1,0:T(8,128)(2,1)}), bf16[128,1024]{1,0:T(8,128)(2,1)}) %reduce-scatter.2.cloned.1.call-update) | async-done | bytes 262160 | tf_op jit(solution)/shard_map/reduce_scatter | solution.py:148
  212.6 4.9 %psum.28 = f32[128]{0:T(128)S(1)} all-reduce(f32[128]{0:T(128)S(1)} %get-tuple-element.13), channel_id=1, replica_groups=mesh['rep'=2,'ep'=8,'tp'=2] {'tp'}, use_global_device_ids=true, to_apply=%region_4.5 | all-reduce | flops 128 | bytes 1024 | tf_op jit(solution)/shard_map/psum | solution.py:155
  217.7 3.9 scatter_custom_fusion
  221.6 15.2 %all-to-all-done.3 = bf16[8,2,73728]{2,1,0:T(2,128)(2,1)S(1)} async-done(((bf16[8,2,73728]{2,1,0:T(2,128)(2,1)}), bf16[8,2,73728]{2,1,0:T(2,128)(2,1)S(1)}, u32[]{:S(2)}, u32[]{:S(2)}) %all-to-all-start.3) | async-done | bytes 2359328 | tf_op jit(solution)/shard_map/all_to_all | solution.py:113
  236.7 4.3 all-to-all-start
  241.3 3.8 scatter_custom_fusion.1
  245.1 33.8 %all-to-all-done = bf16[8,2,48,1024]{3,2,1,0:T(8,128)(2,1)} async-done(((bf16[8,2,48,1024]{3,2,1,0:T(8,128)(2,1)}), bf16[8,2,48,1024]{3,2,1,0:T(8,128)(2,1)}, u32[]{:S(2)}, u32[]{:S(2)}) %all-to-all-start) | async-done | bytes 1572896 | tf_op jit(solution)/shard_map/all_to_all | solution.py:89
  278.9 4.3 all-to-all-start.4
  283.4 4.6 reshape.322
  288.0 14.8 %reduce.4 = bf16[8,147456]{1,0:T(8,128)(2,1)S(1)} reduce(bf16[8,1,147456]{2,1,0:T(2,128)(2,1)} %reshape.322, bf16[]{:T(256)} %constant.67), dimensions={1}, to_apply=%all_to_all.29.reduce_sub_computation | reduce | bytes 4718594 | tf_op jit(solution)/shard_map/all_to_all | solution.py:113
  305.4 6.0 %broadcast_select_fusion = bf16[2,3,1024,384]{3,2,1,0:T(8,128)(2,1)} fusion(bf16[2,3,1024,384]{3,2,1,0:T(8,128)(2,1)} %param.19, pred[2]{0:T(512)(128)(4,1)S(1)} %get-tuple-element.8, bf16[3,1024,384]{2,1,0:T(8,128)(2,1)} %broadcast_in_dim.207), kind=kLoop, calls=%fused_computation.14 | loop fusion | flops 2359296 | bytes 11796482 | tf_op jit(solution)/shard_map/jit(_where)/select_n | solution.py:115
  311.4 3.8 fusion.33
  315.2 5.8 %all-to-all-done.4 = bf16[8,2,48,1024]{3,2,1,0:T(8,128)(2,1)} async-done(((bf16[8,2,48,1024]{3,2,1,0:T(8,128)(2,1)}), bf16[8,2,48,1024]{3,2,1,0:T(8,128)(2,1)}, u32[]{:S(2)}, u32[]{:S(2)}) %all-to-all-start.4) | async-done | bytes 1572896 | tf_op jit(solution)/shard_map/all_to_all | solution.py:89
  321.0 4.8 fusion.38
  325.8 67.7 %all-reduce.3.cloned.1.call-done = (bf16[8,2,48,2,384]{4,2,0,1,3:T(8,128)(2,1)}, bf16[8,2,48,2,384]{4,2,3,0,1:T(8,128)(2,1)}) async-done(((bf16[8,2,48,2,384]{4,2,0,1,3:T(8,128)(2,1)}, bf16[8,2,48,2,384]{4,2,3,0,1:T(8,128)(2,1)}), (bf16[8,2,48,2,384]{4,2,0,1,3:T(8,128)(2,1)}, bf16[8,2,48,2,384]{4,2,3,0,1:T(8,128)(2,1)})) %all-reduce.3.cloned.1.call-update) | async-done | bytes 2359312 | tf_op jit(solution)/shard_map/psum | solution.py:60
  398.7 4.7 all-to-all-start.5
  407.5 33.7 %all-to-all-done.5 = bf16[8,2,48,1024]{3,2,1,0:T(8,128)(2,1)S(1)} async-done(((bf16[8,2,48,1024]{3,2,1,0:T(8,128)(2,1)}), bf16[8,2,48,1024]{3,2,1,0:T(8,128)(2,1)S(1)}, u32[]{:S(2)}, u32[]{:S(2)}) %all-to-all-start.5) | async-done | bytes 1572896 | tf_op jit(solution)/shard_map/all_to_all | solution.py:65
  441.2 3.6 all-to-all-start.1
  445.1 5.2 %psum.29 = bf16[128,16]{0,1:T(8,128)(2,1)S(1)} all-reduce(bf16[128,16]{0,1:T(8,128)(2,1)S(1)} %convolution_convert_fusion.3), channel_id=1, replica_groups=mesh['rep'=2,'ep'=8,'tp'=2] {'tp'}, use_global_device_ids=true, to_apply=%region_5.6 | all-reduce | flops 2048 | bytes 8192 | tf_op jit(solution)/shard_map/psum | solution.py:157
  455.3 27.2 %all-to-all-done.1 = bf16[8,2,48,1024]{3,2,1,0:T(8,128)(2,1)S(1)} async-done(((bf16[8,2,48,1024]{3,2,1,0:T(8,128)(2,1)}), bf16[8,2,48,1024]{3,2,1,0:T(8,128)(2,1)S(1)}, u32[]{:S(2)}, u32[]{:S(2)}) %all-to-all-start.1) | async-done | bytes 1572896 | tf_op jit(solution)/shard_map/all_to_all | solution.py:65
  (104 shorter events, 53.0 us)
Async XLA Ops:
  6.5 438.4 %copy-start = (bf16[1024,16]{0,1:T(8,128)(2,1)S(1)}, bf16[1024,16]{0,1:T(8,128)(2,1)}, u32[]{:S(2)}) copy-start(bf16[1024,16]{0,1:T(8,128)(2,1)} %param.18) | copy-start | bytes 98308
  36.0 113.7 %all-to-all-start.2 = ((bf16[8,2,73728]{2,1,0:T(2,128)(2,1)}), bf16[8,2,73728]{2,1,0:T(2,128)(2,1)S(1)}, u32[]{:S(2)}, u32[]{:S(2)}) async-start(bf16[8,2,73728]{2,1,0:T(2,128)(2,1)} %reshape.319), calls=%async_computation.3 | async-start | bytes 4718592 | tf_op jit(solution)/shard_map/all_to_all | solution.py:107
  42.3 147.4 %all-gather.2.cloned.1.call-start = ((), (), s32[]{:S(2)}) async-start(), calls=%async_computation.7 | async-start | bytes 9437184 | tf_op jit(solution)/shard_map/all_gather | solution.py:145
  175.9 6.4 %copy-start.6 = (s32[2,64,8]{1,2,0:T(8,128)S(1)}, s32[2,64,8]{1,2,0:T(8,128)}, u32[]{:S(2)}) copy-start(s32[2,64,8]{1,2,0:T(8,128)} %param.20) | copy-start | bytes 12292
  175.9 6.5 %copy-start.4 = (bf16[1,64,1,256]{3,2,1,0:T(2,128)(2,1)S(1)}, bf16[1,64,1,256]{3,2,1,0:T(2,128)(2,1)}, u32[]{:S(2)}) copy-start(bf16[1,64,1,256]{3,2,1,0:T(2,128)(2,1)} %get-tuple-element.24) | copy-start | bytes 98308
  175.9 60.9 %all-to-all-start.3 = ((bf16[8,2,73728]{2,1,0:T(2,128)(2,1)}), bf16[8,2,73728]{2,1,0:T(2,128)(2,1)S(1)}, u32[]{:S(2)}, u32[]{:S(2)}) async-start(bf16[8,2,73728]{2,1,0:T(2,128)(2,1)} %reshape.321), calls=%async_computation.4 | async-start | bytes 4718592 | tf_op jit(solution)/shard_map/all_to_all | solution.py:113
  182.1 3.0 copy-start.9
  182.1 29.3 %reduce-scatter.2.cloned.1.call-start = ((), (), s32[]{:S(2)}) async-start(), calls=%async_computation.8 | async-start | bytes 786432 | tf_op jit(solution)/shard_map/reduce_scatter | solution.py:148
  189.7 5.9 %copy-start.7 = (s32[16]{0:T(128)S(1)}, s32[16]{0:T(128)}, u32[]{:S(2)}) copy-start(s32[16]{0:T(128)} %param.22) | copy-start | bytes 196
  189.7 5.9 %copy-start.8 = (s32[16]{0:T(128)S(1)}, s32[16]{0:T(128)}, u32[]{:S(2)}) copy-start(s32[16]{0:T(128)} %param.21) | copy-start | bytes 196
  189.7 21.7 %copy-start.5 = (bf16[2,64,1024]{2,1,0:T(8,128)(2,1)S(1)}, bf16[2,64,1024]{2,1,0:T(8,128)(2,1)}, u32[]{:S(2)}) copy-start(bf16[2,64,1024]{2,1,0:T(8,128)(2,1)} %param.12) | copy-start | bytes 786436
  212.6 24.2 %copy-start.1 = (bf16[128,1024]{1,0:T(8,128)(2,1)}, bf16[128,1024]{1,0:T(8,128)(2,1)S(1)}, u32[]{:S(2)}) copy-start(bf16[128,1024]{1,0:T(8,128)(2,1)S(1)} %get-tuple-element.14) | copy-start | bytes 786436
  236.7 42.1 %all-to-all-start = ((bf16[8,2,48,1024]{3,2,1,0:T(8,128)(2,1)}), bf16[8,2,48,1024]{3,2,1,0:T(8,128)(2,1)}, u32[]{:S(2)}, u32[]{:S(2)}) async-start(bf16[8,2,48,1024]{3,2,1,0:T(8,128)(2,1)} %bitcast.175), calls=%async_computation.1 | async-start | bytes 3145728 | tf_op jit(solution)/shard_map/all_to_all | solution.py:89
  278.9 42.1 %all-to-all-start.4 = ((bf16[8,2,48,1024]{3,2,1,0:T(8,128)(2,1)}), bf16[8,2,48,1024]{3,2,1,0:T(8,128)(2,1)}, u32[]{:S(2)}, u32[]{:S(2)}) async-start(bf16[8,2,48,1024]{3,2,1,0:T(8,128)(2,1)} %bitcast.174), calls=%async_computation.5 | async-start | bytes 3145728 | tf_op jit(solution)/shard_map/all_to_all | solution.py:89
  283.2 110.3 %all-reduce.3.cloned.1.call-start = ((), (), s32[]{:S(2)}) async-start(), calls=%async_computation.9 | async-start | bytes 4718592 | tf_op jit(solution)/shard_map/psum | solution.py:60
  302.9 8.5 %slice-start = ((s8[4718592]{0:T(1024)(128)(4,1)}), s8[524288]{0:T(1024)(128)(4,1)S(1)}, s32[]{:S(2)}) async-start(s8[4718592]{0:T(1024)(128)(4,1)} %bitcast.171), calls=%async_computation.10 | async-start | bytes 1048576
  305.4 6.0 %slice-start.1 = ((s8[4718592]{0:T(1024)(128)(4,1)}), s8[4194304]{0:T(1024)(128)(4,1)S(1)}, s32[]{:S(2)}) async-start(s8[4718592]{0:T(1024)(128)(4,1)} %bitcast.171), calls=%async_computation.11 | async-start | bytes 8388608
  398.7 4.7 copy-start.3
  398.7 42.5 %all-to-all-start.5 = ((bf16[8,2,48,1024]{3,2,1,0:T(8,128)(2,1)}), bf16[8,2,48,1024]{3,2,1,0:T(8,128)(2,1)S(1)}, u32[]{:S(2)}, u32[]{:S(2)}) async-start(bf16[8,2,48,1024]{3,2,1,0:T(8,128)(2,1)} %copy.120), calls=%async_computation.6 | async-start | bytes 3145728 | tf_op jit(solution)/shard_map/all_to_all | solution.py:65
  441.2 41.3 %all-to-all-start.1 = ((bf16[8,2,48,1024]{3,2,1,0:T(8,128)(2,1)}), bf16[8,2,48,1024]{3,2,1,0:T(8,128)(2,1)S(1)}, u32[]{:S(2)}, u32[]{:S(2)}) async-start(bf16[8,2,48,1024]{3,2,1,0:T(8,128)(2,1)} %copy.113), calls=%async_computation.2 | async-start | bytes 3145728 | tf_op jit(solution)/shard_map/all_to_all | solution.py:65
  482.6 2.8 copy-start.2
Sparse Core Ops, SparseCore 0:
  44.7 121.8 all-gather.1
  195.4 16.0 reduce-scatter.1
  325.9 67.5 all-reduce.2
where the time goes:
time: 500 us; the launch traced here: 493 us
  waiting for transfers between devices  286 us (57%)
  local copies, waits for them, and re-layouts  61.7 us (12%)
  other arithmetic  57.2 us (11%)
  matrix products  33.2 us (7%)
  starting transfers between devices  30 us (6%)
  between operations  14.5 us (3%)
  blocking collectives  10.1 us (2%)
    all_to_all x1, waiting for transfers between devices, relocate(): lax.all_to_all(outgoing, 'ep', split_axis=0, concat_axis=0, tiled=True)  86.6 us
    psum x1, waiting for transfers between devices, run_slots(): summed = lax.psum(gate_up.astype(jnp.bfloat16), 'tp').astype(jnp.float32)  67.7 us
    all_to_all x2, waiting for transfers between devices, run_slots(): lax.all_to_all(layer_result, 'ep', split_axis=0, concat_axis=0, tiled=True)  61 us
    all_to_all x2, waiting for transfers between devices, mix_block(): lax.all_to_all(outgoing, 'ep', split_axis=0, concat_axis=0, tiled=True)  39.5 us
    unnamed x32, local copies, waits for them, and re-layouts  25.7 us
    reduce_scatter x1, waiting for transfers between devices, per_device(): lax.psum_scatter(head_terms.astype(jnp.bfloat16), 'tp', scatter_dimension...  15.5 us
    all_to_all x1, other arithmetic, relocate(): lax.all_to_all(outgoing, 'ep', split_axis=0, concat_axis=0, tiled=True)  15.5 us
    all_to_all x1, waiting for transfers between devices, relocate(): lax.all_to_all(picked, 'ep', split_axis=0, concat_axis=0, tiled=True)  15.2 us
  transfers between devices with their start and end apart: 9, of which 8 were waited for; matrix products, arithmetic and copies ran while one was open for 22% of the time, Pallas kernels for 0%

commit v1 on v0

--- a/solution.py
+++ b/solution.py
@@ -57,7 +57,7 @@
     gate_up = jnp.einsum(
         "secq,egqf->secgf", received, weights[:, :2], preferred_element_type=jnp.float32
     )
-    summed = lax.psum(gate_up.astype(jnp.bfloat16), "tp").astype(jnp.float32)
+    summed = jnp.sum(lax.all_gather(gate_up.astype(jnp.bfloat16), "tp"), axis=0).astype(jnp.float32)
     hidden = (jax.nn.silu(summed[:, :, :, 0]) * summed[:, :, :, 1]).astype(jnp.bfloat16)
     layer_result = jnp.einsum(
         "secf,eqf->secq", hidden, weights[:, 2], preferred_element_type=jnp.float32

time: 500 us -> 437 us (0.87)
  waiting for transfers between devices: 286 us -> 221 us
    psum x1 -> x0, waiting for transfers between devices: 67.7 us -> none  [run_slots(): summed = lax.psum(gate_up.astype(jnp.bfloat16), 'tp').astype(jnp.float32)]
    all_gather x0 -> x2, waiting for transfers between devices: none -> 30.7 us  [run_slots(): lax.all_gather(gate_up.astype(jnp.bfloat16), 'tp')]
    all_to_all x2, waiting for transfers between devices: 61 us -> 32.2 us  [run_slots(): lax.all_to_all(layer_result, 'ep', split_axis=0, concat_axis=0, tiled=True)]
    unnamed x32 -> x30, local copies, waits for them, and re-layouts: 25.7 us -> 27.8 us
  transfers between devices with their start and end apart: 9 -> 10, of which waited for: 8 -> 9; matrix products, arithmetic and copies ran while one was open for 22% -> 28% of each run, Pallas kernels for 0% -> 0%
where the time goes in v1:
time: 437 us; the launch traced here: 430 us
  waiting for transfers between devices  221 us (51%)
  local copies, waits for them, and re-layouts  63.9 us (15%)
  other arithmetic  57.4 us (13%)
  matrix products  33.3 us (8%)
  starting transfers between devices  29.7 us (7%)
  between operations  14.4 us (3%)
  blocking collectives  9.87 us (2%)
    all_to_all x1, waiting for transfers between devices, relocate(): lax.all_to_all(outgoing, 'ep', split_axis=0, concat_axis=0, tiled=True)  86.6 us
    all_to_all x2, waiting for transfers between devices, mix_block(): lax.all_to_all(outgoing, 'ep', split_axis=0, concat_axis=0, tiled=True)  40.3 us
    all_to_all x2, waiting for transfers between devices, run_slots(): lax.all_to_all(layer_result, 'ep', split_axis=0, concat_axis=0, tiled=True)  32.2 us
    all_gather x2, waiting for transfers between devices, run_slots(): lax.all_gather(gate_up.astype(jnp.bfloat16), 'tp')  30.7 us
    unnamed x30, local copies, waits for them, and re-layouts  27.8 us
    reduce_scatter x1, waiting for transfers between devices, per_device(): lax.psum_scatter(head_terms.astype(jnp.bfloat16), 'tp', scatter_dimension...  15.5 us
    all_to_all x1, other arithmetic, relocate(): lax.all_to_all(outgoing, 'ep', split_axis=0, concat_axis=0, tiled=True)  15.5 us
    all_to_all x1, waiting for transfers between devices, relocate(): lax.all_to_all(picked, 'ep', split_axis=0, concat_axis=0, tiled=True)  15.2 us
  transfers between devices with their start and end apart: 10, of which 9 were waited for; matrix products, arithmetic and copies ran while one was open for 28% of the time, Pallas kernels for 0%

profile of v1, /device:TPU:0, one launch (start us, length us, event | category | flops | bytes accessed | tf_op | source)
XLA Modules:
  0.0 430.0 jit_solution(16037849742900792322)
XLA Ops:
  7.6 4.8 %select_reduce_fusion = bf16[3,1024,384]{2,1,0:T(8,128)(2,1)S(1)} fusion(bf16[2,3,1024,384]{3,2,1,0:T(8,128)(2,1)} %param.19, pred[2]{0:T(512)(128)(4,1)S(1)} %get-tuple-element.7), kind=kLoop, calls=%fused_computation.11 | loop fusion | flops 3538944 | bytes 7077890 | tf_op jit(solution)/shard_map/reduce_sum | solution.py:106
  12.4 3.9 all_to_all.32
  17.0 15.5 %reduce.9 = bf16[8,147456]{1,0:T(8,128)(2,1)S(1)} reduce(bf16[8,1,147456]{2,1,0:T(2,128)(2,1)} %all_to_all.32, bf16[]{:T(256)} %broadcast.258), dimensions={1}, to_apply=%all_to_all.32.reduce_sub_computation | reduce | bytes 4718594 | tf_op jit(solution)/shard_map/all_to_all | solution.py:107
  36.0 6.4 %all-to-all-start.2 = ((bf16[8,2,73728]{2,1,0:T(2,128)(2,1)}), bf16[8,2,73728]{2,1,0:T(2,128)(2,1)S(1)}, u32[]{:S(2)}, u32[]{:S(2)}) async-start(bf16[8,2,73728]{2,1,0:T(2,128)(2,1)} %reshape.321), calls=%async_computation.3 | async-start | bytes 4718592 | tf_op jit(solution)/shard_map/all_to_all | solution.py:107
  53.8 9.2 %fusion.88 = (f32[2,8,128]{2,1,0:T(8,128)}, f32[2,8,128,1152]{2,3,1,0:T(8,128)}) fusion(pred[128,1152]{0,1:T(8,128)(4,1)} %fusion.55, bf16[128,2,8,128]{3,2,1,0:T(8,128)(2,1)S(1)} %bitcast.184, bf16[64,2,128]{2,0,1:T(8,128)(2,1)S(1)} %get-tuple-element.33, bf16[64,2,128]{2,0,1:T(8,128)(2,1)} %get-tuple-element.34, bf16[1024,2,128]{2,0,1:T(8,128)(2,1)} %copy.98), kind=kOutput, calls=%fused_computation.145 | convolution fusion | flops 617546880 | bytes 10706944 | tf_op jit(solution)/shard_map/sub | solution.py:45
  63.0 86.6 %all-to-all-done.2 = bf16[8,2,73728]{2,1,0:T(2,128)(2,1)S(1)} async-done(((bf16[8,2,73728]{2,1,0:T(2,128)(2,1)}), bf16[8,2,73728]{2,1,0:T(2,128)(2,1)S(1)}, u32[]{:S(2)}, u32[]{:S(2)}) %all-to-all-start.2) | async-done | bytes 2359328 | tf_op jit(solution)/shard_map/all_to_all | solution.py:107
  149.6 4.6 %reshape.322 = bf16[8,1,147456]{2,1,0:T(2,128)(2,1)} reshape(bf16[8,2,73728]{2,1,0:T(2,128)(2,1)S(1)} %all-to-all-done.2) | data formatting | bytes 4718592
  154.2 5.4 %copy.162 = bf16[8,1,147456]{2,0,1:T(8,128)(2,1)S(1)} copy(bf16[8,1,147456]{2,1,0:T(2,128)(2,1)} %reshape.322) | data formatting | bytes 4718592
  170.7 5.2 %reshape.323 = bf16[8,2,73728]{2,1,0:T(2,128)(2,1)} reshape(bf16[8,147456]{1,0:T(8,128)(2,1)} %reduce.10) | data formatting | bytes 4718592
  175.9 6.2 %all-to-all-start.3 = ((bf16[8,2,73728]{2,1,0:T(2,128)(2,1)}), bf16[8,2,73728]{2,1,0:T(2,128)(2,1)S(1)}, u32[]{:S(2)}, u32[]{:S(2)}) async-start(bf16[8,2,73728]{2,1,0:T(2,128)(2,1)} %reshape.323), calls=%async_computation.4 | async-start | bytes 4718592 | tf_op jit(solution)/shard_map/all_to_all | solution.py:113
  185.1 4.6 %fusion.39 = bf16[2,128,8,128]{3,1,2,0:T(8,128)(2,1)S(1)} fusion(f32[2,8,128,1152]{2,3,1,0:T(8,128)} %get-tuple-element.30, f32[2,8,128]{2,1,0:T(8,128)S(1)} %copy-done.10, bf16[1152,2,128]{0,2,1:T(8,128)(2,1)S(1)} %concatenate.23), kind=kOutput, calls=%fused_computation.44 | convolution fusion | flops 608960512 | bytes 10559488 | tf_op jit(solution)/shard_map/qizo,oqx->zqix/dot_general | solution.py:47
  189.7 5.5 %convolution_convert_fusion = bf16[128,2048]{1,0:T(8,128)(2,1)} fusion(bf16[128,2048]{0,1:T(8,128)(2,1)S(1)} %bitcast.182, bf16[2048,2048]{1,0:T(8,128)(2,1)} %all-gather.6.cloned.1.call-done), kind=kOutput, calls=%fused_computation.22 | convolution fusion | flops 1074003968 | bytes 9437184 | tf_op jit(solution)/shard_map/dot_general | solution.py:143
  195.9 15.5 %reduce-scatter.2.cloned.1.call-done = bf16[128,1024]{1,0:T(8,128)(2,1)} async-done(((bf16[128,2048]{1,0:T(8,128)(2,1)}), bf16[128,1024]{1,0:T(8,128)(2,1)}) %reduce-scatter.2.cloned.1.call-update) | async-done | bytes 262160 | tf_op jit(solution)/shard_map/reduce_scatter | solution.py:148
  212.6 4.9 %psum.14 = f32[128]{0:T(128)S(1)} all-reduce(f32[128]{0:T(128)S(1)} %get-tuple-element.11), channel_id=1, replica_groups=mesh['rep'=2,'ep'=8,'tp'=2] {'tp'}, use_global_device_ids=true, to_apply=%region_4.5 | all-reduce | flops 128 | bytes 1024 | tf_op jit(solution)/shard_map/psum | solution.py:155
  217.7 3.8 scatter_custom_fusion.1
  221.5 15.2 %all-to-all-done.3 = bf16[8,2,73728]{2,1,0:T(2,128)(2,1)S(1)} async-done(((bf16[8,2,73728]{2,1,0:T(2,128)(2,1)}), bf16[8,2,73728]{2,1,0:T(2,128)(2,1)S(1)}, u32[]{:S(2)}, u32[]{:S(2)}) %all-to-all-start.3) | async-done | bytes 2359328 | tf_op jit(solution)/shard_map/all_to_all | solution.py:113
  236.7 4.3 all-to-all-start.4
  241.2 4.6 %reshape.324 = bf16[8,1,147456]{2,1,0:T(2,128)(2,1)} reshape(bf16[8,2,73728]{2,1,0:T(2,128)(2,1)S(1)} %all-to-all-done.3) | data formatting | bytes 4718592
  245.8 14.8 %reduce.6 = bf16[8,147456]{1,0:T(8,128)(2,1)S(1)} reduce(bf16[8,1,147456]{2,1,0:T(2,128)(2,1)} %reshape.324, bf16[]{:T(256)} %constant.69), dimensions={1}, to_apply=%all_to_all.29.reduce_sub_computation | reduce | bytes 4718594 | tf_op jit(solution)/shard_map/all_to_all | solution.py:113
  263.2 4.0 scatter_custom_fusion
  267.2 11.7 %all-to-all-done.4 = bf16[8,2,48,1024]{3,2,1,0:T(8,128)(2,1)} async-done(((bf16[8,2,48,1024]{3,2,1,0:T(8,128)(2,1)}), bf16[8,2,48,1024]{3,2,1,0:T(8,128)(2,1)}, u32[]{:S(2)}, u32[]{:S(2)}) %all-to-all-start.4) | async-done | bytes 1572896 | tf_op jit(solution)/shard_map/all_to_all | solution.py:89
  278.8 4.3 %all-to-all-start = ((bf16[8,2,48,1024]{3,2,1,0:T(8,128)(2,1)}), bf16[8,2,48,1024]{3,2,1,0:T(8,128)(2,1)}, u32[]{:S(2)}, u32[]{:S(2)}) async-start(bf16[8,2,48,1024]{3,2,1,0:T(8,128)(2,1)} %bitcast.177), calls=%async_computation.1 | async-start | bytes 3145728 | tf_op jit(solution)/shard_map/all_to_all | solution.py:89
  288.3 3.9 fusion.29
  292.3 28.7 %all-to-all-done = bf16[8,2,48,1024]{3,2,1,0:T(8,128)(2,1)} async-done(((bf16[8,2,48,1024]{3,2,1,0:T(8,128)(2,1)}), bf16[8,2,48,1024]{3,2,1,0:T(8,128)(2,1)}, u32[]{:S(2)}, u32[]{:S(2)}) %all-to-all-start) | async-done | bytes 1572896 | tf_op jit(solution)/shard_map/all_to_all | solution.py:89
  321.0 4.8 %fusion.32 = bf16[8,2,48,2,384]{4,2,3,0,1:T(8,128)(2,1)} fusion(bf16[2,3,1024,384]{3,2,1,0:T(8,128)(2,1)} %param.19, bf16[8,2,48,1024]{3,2,1,0:T(8,128)(2,1)} %all-to-all-done), kind=kOutput, calls=%fused_computation.42 | convolution fusion | flops 1208549376 | bytes 5898240 | tf_op jit(solution)/shard_map/secq,egqf->secgf/dot_general | solution.py:57
  325.7 4.0 all-gather.10.cloned.1.call-done
  335.9 4.6 %all-to-all-start.5 = ((bf16[8,2,48,1024]{3,2,1,0:T(8,128)(2,1)}), bf16[8,2,48,1024]{3,2,1,0:T(8,128)(2,1)S(1)}, u32[]{:S(2)}, u32[]{:S(2)}) async-start(bf16[8,2,48,1024]{3,2,1,0:T(8,128)(2,1)} %copy.116), calls=%async_computation.6 | async-start | bytes 3145728 | tf_op jit(solution)/shard_map/all_to_all | solution.py:65
  340.5 26.7 %all-gather.8.cloned.1.call-done = bf16[16,2,48,2,384]{4,2,3,0,1:T(8,128)(2,1)} async-done(((bf16[8,2,48,2,384]{4,2,3,0,1:T(8,128)(2,1)}), bf16[16,2,48,2,384]{4,2,3,0,1:T(8,128)(2,1)}) %all-gather.8.cloned.1.call-update) | async-done | bytes 2359312 | tf_op jit(solution)/shard_map/all_gather | solution.py:60
  373.6 4.7 %all-to-all-done.5 = bf16[8,2,48,1024]{3,2,1,0:T(8,128)(2,1)S(1)} async-done(((bf16[8,2,48,1024]{3,2,1,0:T(8,128)(2,1)}), bf16[8,2,48,1024]{3,2,1,0:T(8,128)(2,1)S(1)}, u32[]{:S(2)}, u32[]{:S(2)}) %all-to-all-start.5) | async-done | bytes 1572896 | tf_op jit(solution)/shard_map/all_to_all | solution.py:65
  378.3 3.6 all-to-all-start.1
  382.2 4.9 %psum.15 = bf16[128,16]{0,1:T(8,128)(2,1)S(1)} all-reduce(bf16[128,16]{0,1:T(8,128)(2,1)S(1)} %convolution_convert_fusion.3), channel_id=1, replica_groups=mesh['rep'=2,'ep'=8,'tp'=2] {'tp'}, use_global_device_ids=true, to_apply=%region_5.6 | all-reduce | flops 2048 | bytes 8192 | tf_op jit(solution)/shard_map/psum | solution.py:157
  392.1 27.5 %all-to-all-done.1 = bf16[8,2,48,1024]{3,2,1,0:T(8,128)(2,1)S(1)} async-done(((bf16[8,2,48,1024]{3,2,1,0:T(8,128)(2,1)}), bf16[8,2,48,1024]{3,2,1,0:T(8,128)(2,1)S(1)}, u32[]{:S(2)}, u32[]{:S(2)}) %all-to-all-start.1) | async-done | bytes 1572896 | tf_op jit(solution)/shard_map/all_to_all | solution.py:65
  (106 shorter events, 61.1 us)
Async XLA Ops:
  6.5 375.5 %copy-start = (bf16[1024,16]{0,1:T(8,128)(2,1)S(1)}, bf16[1024,16]{0,1:T(8,128)(2,1)}, u32[]{:S(2)}) copy-start(bf16[1024,16]{0,1:T(8,128)(2,1)} %param.18) | copy-start | bytes 98308
  36.0 113.7 %all-to-all-start.2 = ((bf16[8,2,73728]{2,1,0:T(2,128)(2,1)}), bf16[8,2,73728]{2,1,0:T(2,128)(2,1)S(1)}, u32[]{:S(2)}, u32[]{:S(2)}) async-start(bf16[8,2,73728]{2,1,0:T(2,128)(2,1)} %reshape.321), calls=%async_computation.3 | async-start | bytes 4718592 | tf_op jit(solution)/shard_map/all_to_all | solution.py:107
  42.3 147.4 %all-gather.6.cloned.1.call-start = ((), (), s32[]{:S(2)}) async-start(), calls=%async_computation.7 | async-start | bytes 9437184 | tf_op jit(solution)/shard_map/all_gather | solution.py:145
  175.9 6.4 %copy-start.7 = (s32[2,64,8]{1,2,0:T(8,128)S(1)}, s32[2,64,8]{1,2,0:T(8,128)}, u32[]{:S(2)}) copy-start(s32[2,64,8]{1,2,0:T(8,128)} %param.20) | copy-start | bytes 12292
  175.9 6.5 %copy-start.5 = (bf16[1,64,1,256]{3,2,1,0:T(2,128)(2,1)S(1)}, bf16[1,64,1,256]{3,2,1,0:T(2,128)(2,1)}, u32[]{:S(2)}) copy-start(bf16[1,64,1,256]{3,2,1,0:T(2,128)(2,1)} %get-tuple-element.22) | copy-start | bytes 98308
  175.9 60.9 %all-to-all-start.3 = ((bf16[8,2,73728]{2,1,0:T(2,128)(2,1)}), bf16[8,2,73728]{2,1,0:T(2,128)(2,1)S(1)}, u32[]{:S(2)}, u32[]{:S(2)}) async-start(bf16[8,2,73728]{2,1,0:T(2,128)(2,1)} %reshape.323), calls=%async_computation.4 | async-start | bytes 4718592 | tf_op jit(solution)/shard_map/all_to_all | solution.py:113
  182.1 3.0 copy-start.10
  182.1 29.3 %reduce-scatter.2.cloned.1.call-start = ((), (), s32[]{:S(2)}) async-start(), calls=%async_computation.8 | async-start | bytes 786432 | tf_op jit(solution)/shard_map/reduce_scatter | solution.py:148
  189.7 5.9 %copy-start.8 = (s32[16]{0:T(128)S(1)}, s32[16]{0:T(128)}, u32[]{:S(2)}) copy-start(s32[16]{0:T(128)} %param.21) | copy-start | bytes 196
  189.7 5.9 %copy-start.9 = (s32[16]{0:T(128)S(1)}, s32[16]{0:T(128)}, u32[]{:S(2)}) copy-start(s32[16]{0:T(128)} %param.22) | copy-start | bytes 196
  189.7 21.7 %copy-start.6 = (bf16[2,64,1024]{2,1,0:T(8,128)(2,1)S(1)}, bf16[2,64,1024]{2,1,0:T(8,128)(2,1)}, u32[]{:S(2)}) copy-start(bf16[2,64,1024]{2,1,0:T(8,128)(2,1)} %param.12) | copy-start | bytes 786436
  212.6 24.2 %copy-start.3 = (bf16[128,1024]{1,0:T(8,128)(2,1)}, bf16[128,1024]{1,0:T(8,128)(2,1)S(1)}, u32[]{:S(2)}) copy-start(bf16[128,1024]{1,0:T(8,128)(2,1)S(1)} %get-tuple-element.12) | copy-start | bytes 786436
  236.7 42.1 %all-to-all-start.4 = ((bf16[8,2,48,1024]{3,2,1,0:T(8,128)(2,1)}), bf16[8,2,48,1024]{3,2,1,0:T(8,128)(2,1)}, u32[]{:S(2)}, u32[]{:S(2)}) async-start(bf16[8,2,48,1024]{3,2,1,0:T(8,128)(2,1)} %bitcast.176), calls=%async_computation.5 | async-start | bytes 3145728 | tf_op jit(solution)/shard_map/all_to_all | solution.py:89
  263.2 20.0 %copy-start.1 = (bf16[3,1024,384]{2,1,0:T(8,128)(2,1)S(1)}, bf16[3,1024,384]{2,1,0:T(8,128)(2,1)}, u32[]{:S(2)}) copy-start(bf16[3,1024,384]{2,1,0:T(8,128)(2,1)} %broadcast_in_dim.207) | copy-start | bytes 7077892
  278.8 42.1 %all-to-all-start = ((bf16[8,2,48,1024]{3,2,1,0:T(8,128)(2,1)}), bf16[8,2,48,1024]{3,2,1,0:T(8,128)(2,1)}, u32[]{:S(2)}, u32[]{:S(2)}) async-start(bf16[8,2,48,1024]{3,2,1,0:T(8,128)(2,1)} %bitcast.177), calls=%async_computation.1 | async-start | bytes 3145728 | tf_op jit(solution)/shard_map/all_to_all | solution.py:89
  283.2 46.6 %all-gather.10.cloned.1.call-start = ((), (), s32[]{:S(2)}) async-start(), calls=%async_computation.10 | async-start | bytes 3538944 | tf_op jit(solution)/shard_map/all_gather | solution.py:60
  286.2 2.1 copy-start.2
  292.2 75.0 %all-gather.8.cloned.1.call-start = ((), (), s32[]{:S(2)}) async-start(), calls=%async_computation.9 | async-start | bytes 3538944 | tf_op jit(solution)/shard_map/all_gather | solution.py:60
  335.9 42.4 %all-to-all-start.5 = ((bf16[8,2,48,1024]{3,2,1,0:T(8,128)(2,1)}), bf16[8,2,48,1024]{3,2,1,0:T(8,128)(2,1)S(1)}, u32[]{:S(2)}, u32[]{:S(2)}) async-start(bf16[8,2,48,1024]{3,2,1,0:T(8,128)(2,1)} %copy.116), calls=%async_computation.6 | async-start | bytes 3145728 | tf_op jit(solution)/shard_map/all_to_all | solution.py:65
  378.3 41.3 %all-to-all-start.1 = ((bf16[8,2,48,1024]{3,2,1,0:T(8,128)(2,1)}), bf16[8,2,48,1024]{3,2,1,0:T(8,128)(2,1)S(1)}, u32[]{:S(2)}, u32[]{:S(2)}) async-start(bf16[8,2,48,1024]{3,2,1,0:T(8,128)(2,1)} %copy.109), calls=%async_computation.2 | async-start | bytes 3145728 | tf_op jit(solution)/shard_map/all_to_all | solution.py:65
  419.6 2.8 copy-start.4
Sparse Core Ops, SparseCore 0:
  44.7 121.8 all-gather.5
  195.4 16.0 reduce-scatter.1
  292.4 37.3 all-gather.9
  331.1 36.0 all-gather.7
